TPU v7x, 512 devices: a whole 4x4x16 slice. The times are simulated.
512 devices in a mesh: dp: 16 (over y, z_hi), seq: 32 (over z_lo, x, core).
Axes of the slice: x: 4, y: 4, z: 16 (z_hi: 4, z_lo: 4; z = z_hi * 4 + z_lo), core: 2. Of those that a mesh axis runs over, the one named last changes fastest.
Arguments:
- tokens: bfloat16 [1024, 64, 1152], P(('dp', 'seq')), may hold values from -6 to 6
- spatial_qkv: bfloat16 [1024, 64, 1728], P(('dp', 'seq')), may hold values from -6 to 6
- wo_spatial: bfloat16 [576, 1152], replicated, may hold values from -0.25 to 0.25
- w_temporal: bfloat16 [1152, 1728], P(None, 'dp'), may hold values from -0.1875 to 0.1875
- wo_temporal: bfloat16 [576, 1152], replicated, may hold values from -0.25 to 0.25
- cotangent: bfloat16 [1024, 64, 1152], P(('dp', 'seq')), may hold values from -24 to 24
Outputs:
- block_out: bfloat16 [1024, 64, 1152], P(('dp', 'seq'))
- tokens_grad: bfloat16 [1024, 64, 1152], P(('dp', 'seq'))
- spatial_qkv_grad: bfloat16 [1024, 64, 1728], P(('dp', 'seq'))
- wo_spatial_grad: float32 [576, 1152], P('seq', 'dp')
- wo_temporal_grad: float32 [576, 1152], P('seq', 'dp')
All inputs are finite; a program needn't handle non-finite values.
Results may differ from a plain program's by a relative error of at most 0.038.
Values may be sent and summed in bfloat16 or wider, within the bound.
A program may use at most 64 MiB of HBM per device.

v0:
```python
import math
import jax
import jax.numpy as jnp
from jax import lax
from jax.sharding import PartitionSpec as P

DH = 72
FRAMES = 16


def split_three(packed):
    inner_width = packed.shape[-1] // 3
    return (
        packed[..., :inner_width],
        packed[..., inner_width : 2 * inner_width],
        packed[..., 2 * inner_width :],
    )


def head_view(matrix):
    batch_size, length, inner_width = matrix.shape
    return matrix.reshape(batch_size, length, inner_width // DH, DH)


def attention_weights_of(query_heads, key_heads):
    scores = jnp.einsum(
        "blhd,bmhd->bhlm", query_heads, key_heads, preferred_element_type=jnp.float32
    ) * (1.0 / math.sqrt(DH))
    return jax.nn.softmax(scores, axis=-1)


def attention(queries, key_rows, values):
    batch_size, length, inner_width = queries.shape
    weights_full = attention_weights_of(head_view(queries), head_view(key_rows))
    rounded = weights_full.astype(jnp.bfloat16)
    output = jnp.einsum(
        "bhlm,bmhd->blhd", rounded, head_view(values), preferred_element_type=jnp.float32
    )
    return output.reshape(batch_size, length, inner_width).astype(jnp.bfloat16)


def attention_grad(queries, key_rows, values, output_grad):
    batch_size, length, inner_width = queries.shape
    query_heads = head_view(queries)
    key_heads = head_view(key_rows)
    value_heads = head_view(values)
    grad_heads = head_view(output_grad)
    weights_full = attention_weights_of(query_heads, key_heads)
    rounded = weights_full.astype(jnp.bfloat16)
    value_grad = jnp.einsum(
        "bhlm,blhd->bmhd", rounded, grad_heads, preferred_element_type=jnp.float32
    )
    weight_grad = jnp.einsum(
        "blhd,bmhd->bhlm", grad_heads, value_heads, preferred_element_type=jnp.float32
    )
    centered = weight_grad - jnp.sum(weights_full * weight_grad, axis=-1, keepdims=True)
    score_grad = (weights_full * centered * (1.0 / math.sqrt(DH))).astype(jnp.bfloat16)
    query_grad = jnp.einsum(
        "bhlm,bmhd->blhd", score_grad, key_heads, preferred_element_type=jnp.float32
    )
    key_grad = jnp.einsum(
        "bhlm,blhd->bmhd", score_grad, query_heads, preferred_element_type=jnp.float32
    )
    joined = [
        part_grad.reshape(batch_size, length, inner_width)
        for part_grad in (query_grad, key_grad, value_grad)
    ]
    return jnp.concatenate(joined, axis=-1).astype(jnp.bfloat16)


def to_clips(matrix, clip_count):
    frame_total, patch_share, channels = matrix.shape
    grouped = matrix.reshape(clip_count, FRAMES, patch_share, channels).transpose(0, 2, 1, 3)
    return grouped.reshape(clip_count * patch_share, FRAMES, channels)


def from_clips(matrix, clip_count):
    batch_rows, frame_count, channels = matrix.shape
    patch_share = batch_rows // clip_count
    grouped = matrix.reshape(clip_count, patch_share, frame_count, channels).transpose(0, 2, 1, 3)
    return grouped.reshape(clip_count * frame_count, patch_share, channels)


def times_transposed(left, right):
    return lax.dot_general(
        left, right, (((1,), (1,)), ((), ())), preferred_element_type=jnp.float32
    )


def transposed_times(left, right):
    return lax.dot_general(
        left, right, (((0,), (0,)), ((), ())), preferred_element_type=jnp.float32
    )


def forward_project(hidden_rows, weight_shard):
    return jnp.dot(
        hidden_rows,
        lax.all_gather(weight_shard, "dp", axis=1, tiled=True),
        preferred_element_type=jnp.float32,
    )


def backward_project(grad_rows, weight_shard):
    return times_transposed(grad_rows, lax.all_gather(weight_shard, "dp", axis=1, tiled=True))


def shards(tokens, spatial_qkv, wo_spatial, w_temporal, wo_temporal, cotangent):
    frames_dev, patches, feature_width = tokens.shape
    row_total = frames_dev * patches
    seq_devices = lax.axis_size("seq")
    clip_count = frames_dev * seq_devices // FRAMES
    spatial_query, spatial_keys, spatial_values = split_three(spatial_qkv)
    spatial_out = attention(spatial_query, spatial_keys, spatial_values)
    spatial_rows = spatial_out.reshape(row_total, -1)
    hidden_rows = (
        tokens.reshape(row_total, feature_width).astype(jnp.float32)
        + jnp.dot(spatial_rows, wo_spatial, preferred_element_type=jnp.float32)
    ).astype(jnp.bfloat16)
    frame_qkv = (
        forward_project(hidden_rows, w_temporal)
        .astype(jnp.bfloat16)
        .reshape(frames_dev, patches, -1)
    )
    patch_qkv = lax.all_to_all(frame_qkv, "seq", split_axis=1, concat_axis=0, tiled=True)
    temporal_query, temporal_keys, temporal_values = split_three(to_clips(patch_qkv, clip_count))
    patch_out = from_clips(attention(temporal_query, temporal_keys, temporal_values), clip_count)
    temporal_out = lax.all_to_all(patch_out, "seq", split_axis=0, concat_axis=1, tiled=True)
    temporal_rows = temporal_out.reshape(row_total, -1)
    block_out = (
        hidden_rows.astype(jnp.float32)
        + jnp.dot(temporal_rows, wo_temporal, preferred_element_type=jnp.float32)
    ).astype(jnp.bfloat16)
    grad_rows = cotangent.reshape(row_total, feature_width)
    out_grad = (
        times_transposed(grad_rows, wo_temporal)
        .astype(jnp.bfloat16)
        .reshape(frames_dev, patches, -1)
    )
    temporal_part = transposed_times(temporal_rows, grad_rows).astype(jnp.bfloat16)
    patch_out_grad = lax.all_to_all(out_grad, "seq", split_axis=1, concat_axis=0, tiled=True)
    clip_qkv_grad = attention_grad(
        temporal_query, temporal_keys, temporal_values, to_clips(patch_out_grad, clip_count)
    )
    patch_qkv_grad = from_clips(clip_qkv_grad, clip_count)
    frame_qkv_grad = lax.all_to_all(patch_qkv_grad, "seq", split_axis=0, concat_axis=1, tiled=True)
    projection_grad = backward_project(frame_qkv_grad.reshape(row_total, -1), w_temporal).astype(
        jnp.bfloat16
    )
    tokens_grad = (grad_rows.astype(jnp.float32) + projection_grad.astype(jnp.float32)).astype(
        jnp.bfloat16
    )
    spatial_out_grad = (
        times_transposed(tokens_grad, wo_spatial)
        .astype(jnp.bfloat16)
        .reshape(frames_dev, patches, -1)
    )
    spatial_part = transposed_times(spatial_rows, tokens_grad).astype(jnp.bfloat16)
    spatial_qkv_grad = attention_grad(spatial_query, spatial_keys, spatial_values, spatial_out_grad)
    seq_sums = (
        lax.psum_scatter(spatial_part, "seq", scatter_dimension=0, tiled=True).astype(jnp.float32),
        lax.psum_scatter(temporal_part, "seq", scatter_dimension=0, tiled=True).astype(jnp.float32),
    )
    spatial_weight_grad, temporal_weight_grad = (
        lax.psum_scatter(
            seq_sums[0].astype(jnp.bfloat16), "dp", scatter_dimension=1, tiled=True
        ).astype(jnp.float32),
        lax.psum_scatter(
            seq_sums[1].astype(jnp.bfloat16), "dp", scatter_dimension=1, tiled=True
        ).astype(jnp.float32),
    )
    return (
        block_out.reshape(frames_dev, patches, feature_width),
        tokens_grad.reshape(frames_dev, patches, feature_width),
        spatial_qkv_grad,
        spatial_weight_grad,
        temporal_weight_grad,
    )


def solution(mesh):
    placed = (
        P(("dp", "seq"), None, None),
        P(("dp", "seq"), None, None),
        P(),
        P(None, "dp"),
        P(),
        P(("dp", "seq"), None, None),
    )
    return jax.shard_map(
        shards,
        mesh=mesh,
        in_specs=placed,
        out_specs=(
            P(("dp", "seq"), None, None),
            P(("dp", "seq"), None, None),
            P(("dp", "seq"), None, None),
            P("seq", "dp"),
            P("seq", "dp"),
        ),
        check_vma=False,
    )
```

profile of v0, /device:TPU:2, one launch (start us, length us, event | category | flops | bytes accessed | tf_op | source)
XLA Modules:
  0.0 741.1 jit_solution(11731465842137330203)
XLA Ops:
  11.0 10.1 %all-to-all-start.2 = ((bf16[2,64,576]{2,0,1:T(2,128)(2,1)}), bf16[2,64,576]{2,0,1:T(2,128)(2,1)}, u32[]{:S(2)}, u32[]{:S(2)}) async-start(bf16[2,64,576]{2,0,1:T(2,128)(2,1)} %copy.76), calls=%async_computation.2 | async-start | bytes 327680 | tf_op jit(solution)/shard_map/all_to_all | solution.py:141
  23.3 2.4 fusion.21
  27.4 121.9 %all-gather.3.cloned.1.call-done = bf16[16,108,1152]{2,1,0:T(8,128)(2,1)} async-done(((bf16[1,108,1152]{2,1,0:T(8,128)(2,1)}), bf16[16,108,1152]{2,1,0:T(8,128)(2,1)}) %all-gather.3.cloned.1.call-update) | async-done | bytes 3981328 | tf_op jit(solution)/shard_map/all_gather | solution.py:99
  149.4 4.8 reshape.139
  154.2 4.1 convolution_convert_fusion.3
  160.8 5.0 all-to-all-start
  167.5 1.9 reshape_reshape.6
  169.4 9.7 %all-to-all-done = bf16[2,64,1728]{2,0,1:T(2,128)(2,1)S(1)} async-done(((bf16[2,64,1728]{2,0,1:T(2,128)(2,1)}), bf16[2,64,1728]{2,0,1:T(2,128)(2,1)S(1)}, u32[]{:S(2)}, u32[]{:S(2)}) %all-to-all-start) | async-done | bytes 442400 | tf_op jit(solution)/shard_map/all_to_all | solution.py:125
  180.2 1.9 reshape.123
  185.4 2.2 fusion.128
  187.6 2.3 fusion.22
  193.5 5.9 all-to-all-start.1
  199.4 2.2 fusion.25
  203.5 1.9 fusion.24
  206.3 2.0 fusion.23
  211.8 8.0 %all-to-all-start.3 = ((bf16[64,2,1728]{2,1,0:T(2,128)(2,1)}), bf16[64,2,1728]{2,1,0:T(2,128)(2,1)}, u32[]{:S(2)}, u32[]{:S(2)}) async-start(bf16[64,2,1728]{2,1,0:T(2,128)(2,1)} %copy.89), calls=%async_computation.3 | async-start | bytes 917504 | tf_op jit(solution)/shard_map/all_to_all | solution.py:146
  219.8 1.7 copy.198
  224.2 8.9 %all-to-all-done.3 = bf16[64,2,1728]{2,1,0:T(2,128)(2,1)} async-done(((bf16[64,2,1728]{2,1,0:T(2,128)(2,1)}), bf16[64,2,1728]{2,1,0:T(2,128)(2,1)}, u32[]{:S(2)}, u32[]{:S(2)}) %all-to-all-start.3) | async-done | bytes 442400 | tf_op jit(solution)/shard_map/all_to_all | solution.py:146
  233.1 2.1 copy.197
  235.2 2.2 reshape.132
  237.4 3.1 fusion.6
  248.7 1.7 fusion.26
  250.8 275.0 %all-reduce.9.cloned.1.call-done = (bf16[576,1152]{1,0:T(8,128)(2,1)}, bf16[576,1152]{1,0:T(8,128)(2,1)}) async-done(((bf16[576,1152]{1,0:T(8,128)(2,1)}, bf16[576,1152]{1,0:T(8,128)(2,1)}), (bf16[576,1152]{1,0:T(8,128)(2,1)}, bf16[576,1152]{1,0:T(8,128)(2,1)})) %all-reduce.9.cloned.1.call-update) | async-done | bytes 2654224
  531.1 200.7 %all-reduce.11.cloned.1.call-done = (bf16[18,1152]{1,0:T(8,128)(2,1)}, bf16[18,1152]{1,0:T(8,128)(2,1)}) async-done(((bf16[18,1152]{1,0:T(8,128)(2,1)}, bf16[18,1152]{1,0:T(8,128)(2,1)}), (bf16[18,1152]{1,0:T(8,128)(2,1)}, bf16[18,1152]{1,0:T(8,128)(2,1)})) %all-reduce.11.cloned.1.call-update) | async-done | bytes 82960
  (98 shorter events, 44.1 us)
Async XLA Ops:
  7.2 1.3 copy-start
  7.2 142.2 %all-gather.3.cloned.1.call-start = ((), (), s32[]{:S(2)}) async-start(), calls=%async_computation.4 | async-start | bytes 4386816 | tf_op jit(solution)/shard_map/all_gather | solution.py:99
  8.5 12.6 %copy-start.11 = (bf16[2,64,1728]{2,1,0:T(8,128)(2,1)S(1)}, bf16[2,64,1728]{2,1,0:T(8,128)(2,1)}, u32[]{:S(2)}) copy-start(bf16[2,64,1728]{2,1,0:T(8,128)(2,1)} %param.7) | copy-start | bytes 1327108
  11.0 149.7 %all-to-all-start.2 = ((bf16[2,64,576]{2,0,1:T(2,128)(2,1)}), bf16[2,64,576]{2,0,1:T(2,128)(2,1)}, u32[]{:S(2)}, u32[]{:S(2)}) async-start(bf16[2,64,576]{2,0,1:T(2,128)(2,1)} %copy.76), calls=%async_computation.2 | async-start | bytes 327680 | tf_op jit(solution)/shard_map/all_to_all | solution.py:141
  21.5 1.8 copy-start.13
  21.8 1.5 copy-start.15
  22.1 1.2 copy-start.8
  23.3 3.7 copy-start.1
  23.3 3.7 copy-start.12
  27.0 127.2 %copy-start.4 = (bf16[128,576]{1,0:T(8,128)(2,1)}, bf16[128,576]{1,0:T(8,128)(2,1)S(1)}, u32[]{:S(2)}) copy-start(bf16[128,576]{1,0:T(8,128)(2,1)S(1)} %convert_element_type.94) | copy-start | bytes 442372
  160.8 18.3 %all-to-all-start = ((bf16[2,64,1728]{2,0,1:T(2,128)(2,1)}), bf16[2,64,1728]{2,0,1:T(2,128)(2,1)S(1)}, u32[]{:S(2)}, u32[]{:S(2)}) async-start(bf16[2,64,1728]{2,0,1:T(2,128)(2,1)} %copy.64), calls=%async_computation | async-start | bytes 917504 | tf_op jit(solution)/shard_map/all_to_all | solution.py:125
  179.5 4.9 copy-start.10
  193.5 18.3 %all-to-all-start.1 = ((bf16[64,2,576]{2,1,0:T(2,128)(2,1)}), bf16[64,2,576]{2,1,0:T(2,128)(2,1)}, u32[]{:S(2)}, u32[]{:S(2)}) async-start(bf16[64,2,576]{2,1,0:T(2,128)(2,1)} %copy.73), calls=%async_computation.1 | async-start | bytes 327680 | tf_op jit(solution)/shard_map/all_to_all | solution.py:128
  210.6 12.0 %copy-start.2 = (bf16[2,64,1152]{2,1,0:T(8,128)(2,1)S(1)}, bf16[2,64,1152]{2,1,0:T(8,128)(2,1)}, u32[]{:S(2)}) copy-start(bf16[2,64,1152]{2,1,0:T(8,128)(2,1)} %param.11) | copy-start | bytes 884740
  211.8 21.3 %all-to-all-start.3 = ((bf16[64,2,1728]{2,1,0:T(2,128)(2,1)}), bf16[64,2,1728]{2,1,0:T(2,128)(2,1)}, u32[]{:S(2)}, u32[]{:S(2)}) async-start(bf16[64,2,1728]{2,1,0:T(2,128)(2,1)} %copy.89), calls=%async_computation.3 | async-start | bytes 917504 | tf_op jit(solution)/shard_map/all_to_all | solution.py:146
  219.8 306.0 %all-reduce.9.cloned.1.call-start = ((), (), s32[]{:S(2)}) async-start(), calls=%async_computation.5 | async-start | bytes 5308416
  222.6 12.7 %copy-start.6 = (bf16[128,576]{1,0:T(8,128)(2,1)}, bf16[128,576]{1,0:T(8,128)(2,1)S(1)}, u32[]{:S(2)}) copy-start(bf16[128,576]{1,0:T(8,128)(2,1)S(1)} %reshape.126) | copy-start | bytes 442372
  237.4 3.1 copy-start.5
  240.5 6.7 copy-start.3
  242.1 3.9 copy-start.7
  242.2 489.6 %all-reduce.11.cloned.1.call-start = ((), (), s32[]{:S(2)}) async-start(), calls=%async_computation.6 | async-start | bytes 221184
  247.2 1.0 copy-start.9
  247.7 1.0 copy-start.16
  248.7 1.7 copy-start.14
Sparse Core Ops, SparseCore 0:
  11.1 138.2 all-gather.2
  242.3 283.4 all-reduce.8
  528.8 202.9 all-reduce.10
where the time goes:
time: 742 us; the launch traced here: 741 us
  waiting for transfers between devices  617 us (83%)
  local copies, waits for them, and re-layouts  43.8 us (6%)
  matrix products  33.1 us (4%)
  starting transfers between devices  29 us (4%)
  between operations  15.5 us (2%)
    unnamed x5, waiting for transfers between devices  476 us
    all_gather x1, waiting for transfers between devices, forward_project(): lax.all_gather(weight_shard, 'dp', axis=1, tiled=True)  122 us
  transfers between devices with their start and end apart: 7, of which 5 were waited for; matrix products, arithmetic and copies ran while one was open for 7% of the time, Pallas kernels for 0%

commit v1 on v0

--- a/solution.py
+++ b/solution.py
@@ -143,7 +143,12 @@
         temporal_query, temporal_keys, temporal_values, to_clips(patch_out_grad, clip_count)
     )
     patch_qkv_grad = from_clips(clip_qkv_grad, clip_count)
-    frame_qkv_grad = lax.all_to_all(patch_qkv_grad, "seq", split_axis=0, concat_axis=1, tiled=True)
+    frame_qkv_grad = jnp.concatenate(
+        lax.all_to_all(
+            jnp.stack(jnp.split(patch_qkv_grad, lax.axis_size("seq"), axis=0)), "seq", 0, 0
+        ),
+        axis=1,
+    )
     projection_grad = backward_project(frame_qkv_grad.reshape(row_total, -1), w_temporal).astype(
         jnp.bfloat16
     )

time: 742 us -> 789 us (1.063)
  local copies, waits for them, and re-layouts: 43.8 us -> 86.8 us
    unnamed x38 -> x73, local copies, waits for them, and re-layouts: 9.97 us -> 54.5 us
  transfers between devices with their start and end apart: 7 -> 7, of which waited for: 5 -> 5; matrix products, arithmetic and copies ran while one was open for 7% -> 11% of each run, Pallas kernels for 0% -> 0%
where the time goes in v1:
time: 789 us; the launch traced here: 786 us
  waiting for transfers between devices  618 us (78%)
  local copies, waits for them, and re-layouts  86.8 us (11%)
  matrix products  34.2 us (4%)
  starting transfers between devices  28.8 us (4%)
  between operations  15.5 us (2%)
    unnamed x5, waiting for transfers between devices  476 us
    all_gather x1, waiting for transfers between devices, forward_project(): lax.all_gather(weight_shard, 'dp', axis=1, tiled=True)  122 us
    unnamed x73, local copies, waits for them, and re-layouts  54.5 us
  transfers between devices with their start and end apart: 7, of which 5 were waited for; matrix products, arithmetic and copies ran while one was open for 11% of the time, Pallas kernels for 0%

profile of v1, /device:TPU:2, one launch (start us, length us, event | category | flops | bytes accessed | tf_op | source)
XLA Modules:
  0.0 785.9 jit_solution(7941023724379906741)
XLA Ops:
  11.0 10.1 %all-to-all-start.2 = ((bf16[2,64,576]{2,0,1:T(2,128)(2,1)}), bf16[2,64,576]{2,0,1:T(2,128)(2,1)}, u32[]{:S(2)}, u32[]{:S(2)}) async-start(bf16[2,64,576]{2,0,1:T(2,128)(2,1)} %copy.76), calls=%async_computation.2 | async-start | bytes 327680 | tf_op jit(solution)/shard_map/all_to_all | solution.py:141
  23.3 2.4 fusion.21
  27.4 122.0 %all-gather.3.cloned.1.call-done = bf16[16,108,1152]{2,1,0:T(8,128)(2,1)} async-done(((bf16[1,108,1152]{2,1,0:T(8,128)(2,1)}), bf16[16,108,1152]{2,1,0:T(8,128)(2,1)}) %all-gather.3.cloned.1.call-update) | async-done | bytes 3981328 | tf_op jit(solution)/shard_map/all_gather | solution.py:99
  149.4 4.9 reshape.138
  154.2 4.1 convolution_convert_fusion.3
  160.8 5.0 all-to-all-start
  167.5 1.9 reshape_reshape.9
  169.4 9.7 %all-to-all-done = bf16[2,64,1728]{2,0,1:T(2,128)(2,1)S(1)} async-done(((bf16[2,64,1728]{2,0,1:T(2,128)(2,1)}), bf16[2,64,1728]{2,0,1:T(2,128)(2,1)S(1)}, u32[]{:S(2)}, u32[]{:S(2)}) %all-to-all-start) | async-done | bytes 442400 | tf_op jit(solution)/shard_map/all_to_all | solution.py:125
  184.4 2.2 fusion.128
  186.6 2.2 fusion.25
  188.8 2.3 fusion.22
  191.1 2.8 fusion.23
  193.9 2.3 fusion.24
  205.1 5.9 all-to-all-start.1
  256.9 7.8 all-to-all-start.3
  266.6 1.6 convolution_convert_fusion
  268.2 9.8 %all-to-all-done.3 = bf16[32,2,2,1728]{3,1,2,0:T(2,128)(2,1)} async-done(((bf16[32,2,2,1728]{3,1,2,0:T(2,128)(2,1)}), bf16[32,2,2,1728]{3,1,2,0:T(2,128)(2,1)}, u32[]{:S(2)}, u32[]{:S(2)}) %all-to-all-start.3) | async-done | bytes 442400 | tf_op jit(solution)/shard_map/all_to_all | solution.py:147
  278.0 2.1 copy.89
  280.2 2.1 reshape_reshape.10
  282.3 3.1 fusion.6
  293.5 1.7 fusion.26
  295.6 275.0 %all-reduce.9.cloned.1.call-done = (bf16[576,1152]{1,0:T(8,128)(2,1)}, bf16[576,1152]{1,0:T(8,128)(2,1)}) async-done(((bf16[576,1152]{1,0:T(8,128)(2,1)}, bf16[576,1152]{1,0:T(8,128)(2,1)}), (bf16[576,1152]{1,0:T(8,128)(2,1)}, bf16[576,1152]{1,0:T(8,128)(2,1)})) %all-reduce.9.cloned.1.call-update) | async-done | bytes 2654224
  572.2 1.6 fusion.27
  576.0 200.7 %all-reduce.11.cloned.1.call-done = (bf16[18,1152]{1,0:T(8,128)(2,1)}, bf16[18,1152]{1,0:T(8,128)(2,1)}) async-done(((bf16[18,1152]{1,0:T(8,128)(2,1)}, bf16[18,1152]{1,0:T(8,128)(2,1)}), (bf16[18,1152]{1,0:T(8,128)(2,1)}, bf16[18,1152]{1,0:T(8,128)(2,1)})) %all-reduce.11.cloned.1.call-update) | async-done | bytes 82960
  (133 shorter events, 87.4 us)
Async XLA Ops:
  7.2 1.3 copy-start
  7.2 142.2 %all-gather.3.cloned.1.call-start = ((), (), s32[]{:S(2)}) async-start(), calls=%async_computation.4 | async-start | bytes 4386816 | tf_op jit(solution)/shard_map/all_gather | solution.py:99
  8.5 12.6 %copy-start.11 = (bf16[2,64,1728]{2,1,0:T(8,128)(2,1)S(1)}, bf16[2,64,1728]{2,1,0:T(8,128)(2,1)}, u32[]{:S(2)}) copy-start(bf16[2,64,1728]{2,1,0:T(8,128)(2,1)} %param.7) | copy-start | bytes 1327108
  11.0 149.8 %all-to-all-start.2 = ((bf16[2,64,576]{2,0,1:T(2,128)(2,1)}), bf16[2,64,576]{2,0,1:T(2,128)(2,1)}, u32[]{:S(2)}, u32[]{:S(2)}) async-start(bf16[2,64,576]{2,0,1:T(2,128)(2,1)} %copy.76), calls=%async_computation.2 | async-start | bytes 327680 | tf_op jit(solution)/shard_map/all_to_all | solution.py:141
  21.5 1.8 copy-start.15
  21.8 1.5 copy-start.17
  22.1 1.2 copy-start.8
  23.3 3.7 copy-start.1
  23.3 3.7 copy-start.13
  27.0 127.3 %copy-start.4 = (bf16[128,576]{1,0:T(8,128)(2,1)}, bf16[128,576]{1,0:T(8,128)(2,1)S(1)}, u32[]{:S(2)}) copy-start(bf16[128,576]{1,0:T(8,128)(2,1)S(1)} %convert_element_type.94) | copy-start | bytes 442372
  160.8 18.3 %all-to-all-start = ((bf16[2,64,1728]{2,0,1:T(2,128)(2,1)}), bf16[2,64,1728]{2,0,1:T(2,128)(2,1)S(1)}, u32[]{:S(2)}, u32[]{:S(2)}) async-start(bf16[2,64,1728]{2,0,1:T(2,128)(2,1)} %copy.64), calls=%async_computation | async-start | bytes 917504 | tf_op jit(solution)/shard_map/all_to_all | solution.py:125
  179.5 3.9 copy-start.10
  191.1 2.8 copy-start.12
  196.2 3.8 copy-start.14
  205.1 51.8 %all-to-all-start.1 = ((bf16[64,2,576]{2,1,0:T(2,128)(2,1)}), bf16[64,2,576]{2,1,0:T(2,128)(2,1)S(1)}, u32[]{:S(2)}, u32[]{:S(2)}) async-start(bf16[64,2,576]{2,1,0:T(2,128)(2,1)} %copy.73), calls=%async_computation.1 | async-start | bytes 327680 | tf_op jit(solution)/shard_map/all_to_all | solution.py:128
  210.9 55.6 %copy-start.2 = (bf16[2,64,1152]{2,1,0:T(8,128)(2,1)S(1)}, bf16[2,64,1152]{2,1,0:T(8,128)(2,1)}, u32[]{:S(2)}) copy-start(bf16[2,64,1152]{2,1,0:T(8,128)(2,1)} %param.11) | copy-start | bytes 884740
  256.9 21.1 %all-to-all-start.3 = ((bf16[32,2,2,1728]{3,1,2,0:T(2,128)(2,1)}), bf16[32,2,2,1728]{3,1,2,0:T(2,128)(2,1)}, u32[]{:S(2)}, u32[]{:S(2)}) async-start(bf16[32,2,2,1728]{3,1,2,0:T(2,128)(2,1)} %constant_dynamic-update-slice_fusion), calls=%async_computation.3 | async-start | bytes 917504 | tf_op jit(solution)/shard_map/all_to_all | solution.py:147
  264.7 306.0 %all-reduce.9.cloned.1.call-start = ((), (), s32[]{:S(2)}) async-start(), calls=%async_computation.5 | async-start | bytes 5308416
  266.5 13.6 %copy-start.6 = (bf16[128,576]{1,0:T(8,128)(2,1)}, bf16[128,576]{1,0:T(8,128)(2,1)S(1)}, u32[]{:S(2)}) copy-start(bf16[128,576]{1,0:T(8,128)(2,1)S(1)} %reshape.125) | copy-start | bytes 442372
  282.3 3.1 copy-start.5
  285.4 6.7 copy-start.3
  287.0 3.9 copy-start.7
  287.0 489.6 %all-reduce.11.cloned.1.call-start = ((), (), s32[]{:S(2)}) async-start(), calls=%async_computation.6 | async-start | bytes 221184
  293.5 1.7 copy-start.16
  (2 other events, 1.9 us)
Sparse Core Ops, SparseCore 0:
  11.1 138.2 all-gather.2
  287.1 283.4 all-reduce.8
  573.6 202.9 all-reduce.10
